TPU v7x, 32 devices: a whole 2x2x4 slice. The times are simulated.
32 devices in a mesh: groups: 2 (over y), obs: 4 (over z), hid: 2 (over x), rep: 2 (over core).
Axes of the slice: x: 2, y: 2, z: 4, core: 2. Of those that a mesh axis runs over, the one named last changes fastest.
Arguments:
- particles: float32 [8, 128, 512], P(('groups', 'obs')), parts along dimension 0, may hold values from -6 to 6
- obs_embed: bfloat16 [32768, 256], P(('groups', 'obs', 'rep')), parts along dimension 0, may hold values from -6 to 6
- step_index: int32 [2], P('groups'), parts along dimension 0, may hold values from 1 to 63
- noise: float32 [8, 128, 512], P('groups', 'obs'), parts along dimension 0, may hold values from -6 to 6
- w_query: bfloat16 [512, 2048], P(None, 'hid'), may hold values from -0.25 to 0.25
- w_key: bfloat16 [256, 2048], P(None, 'hid'), may hold values from -0.375 to 0.375
- w_value: bfloat16 [256, 2048], P(None, 'hid'), may hold values from -0.375 to 0.375
- w_time: bfloat16 [256, 16], P(None, 'hid'), may hold values from -0.375 to 0.375
- w_score: bfloat16 [2048, 512], P('hid'), may hold values from -0.0009765625 to 0.0009765625
- prior_in: bfloat16 [512, 2048], P(None, 'hid'), may hold values from -0.25 to 0.25
- prior_time: bfloat16 [256, 2048], P(None, 'hid'), may hold values from -0.375 to 0.375
- prior_out: bfloat16 [2048, 512], P('hid'), may hold values from -7.6293945e-06 to 7.6293945e-06
Outputs:
- updated: float32 [8, 128, 512], P('groups', 'obs'), parts along dimension 0
- score_total: float32 [8, 128, 512], P('groups', 'obs'), parts along dimension 0
There are 2 independent parts, one for each index of `groups`. A program takes and returns all parts, laid end to end along the dimension named above; an argument that names none is the same for every part. Nothing has to cross between parts.
All inputs are finite; a program needn't handle non-finite values.
Results may differ from a plain program's by a relative error of at most 0.0042.
Values may be sent and summed in bfloat16 or wider, within the bound.
No kernel may reach another device: no remote copies, remote signals or barrier semaphores. Data moves between devices by JAX's collectives and lax.ppermute only.
A program may use at most 64 MiB of HBM per device.

v0:
```python
import math
import jax
import jax.numpy as jnp
from jax import lax
from jax.sharding import PartitionSpec as P

DH = 128
STEPS = 64
SIG_LO = 0.05
SIG_HI = 1.0


def passed_along(shard, axis, by):
    size = lax.axis_size(axis)
    return lax.ppermute(shard, axis, [(i, (i + by) % size) for i in range(size)])


def plan(step_index, feature_count):
    level = step_index[0].astype(jnp.float32)
    growth = math.log(SIG_HI / SIG_LO) / (STEPS - 1)
    sigma_now = SIG_LO * jnp.exp(growth * level)
    sigma_prev = SIG_LO * jnp.exp(growth * (level - 1.0))
    delta = sigma_now * sigma_now - sigma_prev * sigma_prev
    halves = feature_count // 2
    frequency = jnp.exp(-math.log(1000.0) / halves * jnp.arange(halves).astype(jnp.float32))
    angles = 10.0 * jnp.log(sigma_now) * frequency
    features = jnp.concatenate([jnp.sin(angles), jnp.cos(angles)])[None, :].astype(jnp.bfloat16)
    return (features, delta)


def pair_pool(queries, keys, values, head_bias):
    count = queries.shape[0]
    query_heads = queries.reshape(count, -1, DH)
    key_heads = keys.reshape(keys.shape[0], -1, DH)
    value_heads = values.reshape(values.shape[0], -1, DH)
    scores = jnp.einsum("phd,jhd->phj", query_heads, key_heads, preferred_element_type=jnp.float32)
    weights = jax.nn.silu(scores * (1.0 / math.sqrt(DH)) + head_bias[None, :, None]).astype(
        jnp.bfloat16
    )
    pooled = jnp.einsum("phj,jhd->phd", weights, value_heads, preferred_element_type=jnp.float32)
    return pooled.reshape(count, -1)


def on_device(
    particles,
    obs_embed,
    step_index,
    noise,
    w_query,
    w_key,
    w_value,
    w_time,
    w_score,
    prior_in,
    prior_time,
    prior_out,
):
    obs_count = lax.axis_size("obs")
    rep_count = lax.axis_size("rep")
    features, delta = plan(step_index, w_time.shape[0])
    head_bias = jnp.dot(features, w_time, preferred_element_type=jnp.float32)[0]
    keys = jnp.dot(obs_embed, w_key, preferred_element_type=jnp.float32).astype(jnp.bfloat16)
    values = jnp.dot(obs_embed, w_value, preferred_element_type=jnp.float32).astype(jnp.bfloat16)
    home = particles[0]
    block_rows = home.shape[0]
    width = home.shape[1]
    stripe = block_rows // obs_count
    owned = home.reshape(obs_count, stripe, width)
    theta_owner = lax.all_to_all(owned, "obs", split_axis=0, concat_axis=0, tiled=True)
    moving = home.astype(jnp.bfloat16)

    def pool(travel):
        queries = jnp.dot(travel, w_query, preferred_element_type=jnp.float32).astype(jnp.bfloat16)
        return pair_pool(queries, keys, values, head_bias)

    score_weight = w_score.astype(jnp.float32)

    def turn(turn_index, cycle_state):
        arrived = passed_along(cycle_state[0], "obs", 1)
        totals = passed_along(cycle_state[1], "obs", 1)
        return (arrived, totals + pool(arrived))

    cycle_state = lax.fori_loop(0, obs_count - 1, turn, (moving, pool(moving)))
    pieces = cycle_state[1].reshape(obs_count, stripe, -1)
    flat = pieces.reshape(-1, pieces.shape[-1])
    result = jnp.dot(
        flat, score_weight, precision=lax.Precision.HIGHEST, preferred_element_type=jnp.float32
    )
    pieces = result.reshape(pieces.shape[:-1] + (width,))
    received = lax.all_to_all(pieces, "obs", split_axis=0, concat_axis=0, tiled=True)
    summed = jnp.roll(received, 1, axis=0)
    owner_rows = theta_owner.reshape(block_rows, width)
    share = block_rows // rep_count
    start = lax.axis_index("rep") * share
    my_rows = lax.dynamic_slice_in_dim(owner_rows, start, share, 0).astype(jnp.bfloat16)
    prior_pre = jnp.dot(my_rows, prior_in, preferred_element_type=jnp.float32) + jnp.dot(
        features, prior_time, preferred_element_type=jnp.float32
    )
    prior_hidden = jax.nn.silu(prior_pre).astype(jnp.bfloat16)
    prior_part = jnp.dot(prior_hidden, prior_out, preferred_element_type=jnp.float32)
    total_count = obs_embed.shape[0] * obs_count * rep_count
    scores_flat = summed.reshape(block_rows, width)
    current = lax.dynamic_slice_in_dim(scores_flat, start, share, 0)
    scores_flat = lax.dynamic_update_slice_in_dim(
        scores_flat, current - (total_count - 1) * prior_part, start, 0
    )
    score_total = lax.psum(scores_flat, ("hid", "rep")).reshape(obs_count, stripe, width)
    updated = theta_owner + delta * score_total + jnp.sqrt(delta) * noise
    return (updated, score_total)


def solution(mesh):
    in_specs = (
        P(("groups", "obs"), None, None),
        P(("groups", "obs", "rep"), None),
        P("groups"),
        P("groups", "obs", None),
        P(None, "hid"),
        P(None, "hid"),
        P(None, "hid"),
        P(None, "hid"),
        P("hid", None),
        P(None, "hid"),
        P(None, "hid"),
        P("hid", None),
    )
    out_specs = (P("groups", "obs", None), P("groups", "obs", None))
    return jax.shard_map(
        on_device, mesh=mesh, in_specs=in_specs, out_specs=out_specs, check_vma=False
    )
```

profile of v0, /device:TPU:0, one launch (start us, length us, event | category | flops | bytes accessed | tf_op | source)
XLA Modules:
  0.0 154.7 jit_solution(1549332694135412617)
XLA Ops:
  7.2 0.0 copy-start
  8.1 0.3 copy-done
  8.4 0.0 copy-start.4
  8.4 4.3 %convolution_convert_fusion.2 = bf16[2048,1024]{0,1:T(8,128)(2,1)} fusion(bf16[2048,256]{1,0:T(8,128)(2,1)S(1)} %copy-done, bf16[256,1024]{1,0:T(8,128)(2,1)} %param.20), kind=kOutput, calls=%fused_computation.23 | convolution fusion | flops 1075838976 | bytes 5767168 | tf_op jit(solution)/shard_map/dot_general | solution.py:63
  12.8 0.0 copy-done.4
  12.8 0.0 copy-start.2
  12.8 3.3 %convolution_convert_fusion.1 = bf16[2048,1024]{0,1:T(8,128)(2,1)} fusion(bf16[2048,256]{1,0:T(8,128)(2,1)S(1)} %copy-done, bf16[256,1024]{1,0:T(8,128)(2,1)S(1)} %copy-done.4), kind=kOutput, calls=%fused_computation.22 | convolution fusion | flops 1075838976 | bytes 5767168 | tf_op jit(solution)/shard_map/dot_general | solution.py:62
  16.0 0.0 copy-done.2
  16.1 0.0 copy-start.7
  16.1 0.0 copy-start.1
  16.1 6.5 %copy.19 = bf16[2048,1024]{1,0:T(8,128)(2,1)} copy(bf16[2048,1024]{0,1:T(8,128)(2,1)} %convolution_convert_fusion.1) | data formatting | bytes 8388608 | tf_op jit(solution)/shard_map/while | solution.py:83
  22.6 0.0 copy-done.7
  22.6 0.1 fusion.35
  22.7 0.0 copy-done.1
  22.7 0.3 fusion.21
  23.0 8.8 %fusion.20 = f32[8,128,128]{2,1,0:T(8,128)} fusion(bf16[2048,8,128]{0,2,1:T(8,128)(2,1)} %bitcast.116, bf16[2048,8,128]{0,2,1:T(8,128)(2,1)} %bitcast.115, f32[8]{0:T(128)S(1)} %bitcast.124, bf16[16,8,8,128]{3,2,1,0:T(8,128)(2,1)S(1)} %fusion.21), kind=kOutput, calls=%fused_computation.24 | convolution fusion | flops 1088421888 | bytes 9175072 | tf_op jit(solution)/shard_map/phj,jhd->phd/dot_general | solution.py:40
  31.9 56.9 %while.12 = (s32[]{:T(128)}, bf16[128,512]{1,0:T(8,128)(2,1)S(1)}, f32[128,1024]{0,1:T(8,128)}, bf16[512,1024]{1,0:T(8,128)(2,1)S(1)}, bf16[2048,1024]{1,0:T(8,1...) while((s32[]{:T(128)}, bf16[128,512]{1,0:T(8,128)(2,1)S(1)}, ...), condition=%wide.region_1.2_spmd, body=%wide.region_0.1_spmd.sunk | while | flops 1222901760 | bytes 15073477 | solution.py:83
  31.9 3.0 %collective-permute-start = (bf16[128,512]{1,0:T(8,128)(2,1)S(1)}, bf16[128,512]{1,0:T(8,128)(2,1)S(1)}, u32[]{:S(2)}, u32[]{:S(2)}) collective-permute-start(bf16[128,512]{1,0:T(8,128)(2,1)S(1)} %get-tuple-element.115), channel_id=1, source_target_pairs={{0,4},{4,8},{8,12},{12,0},{1,5},{5,9},{9,13},{13,1},{2,6},{6,10},{... | collective-permute-start | bytes 393224 | tf_op jit(solution)/shard_map/while/body/eval_jaxpr/ppermute | solution.py:15
  34.9 1.6 %collective-permute-start.1 = (f32[128,1024]{0,1:T(8,128)}, f32[128,1024]{0,1:T(8,128)S(1)}, u32[]{:S(2)}, u32[]{:S(2)}) collective-permute-start(f32[128,1024]{0,1:T(8,128)} %get-tuple-element.116), channel_id=1, source_target_pairs={{0,4},{4,8},{8,12},{12,0},{1,5},{5,9},{9,13},{13,1},{2,6},{6,10},{... | collective-permute-start | bytes 1572872 | tf_op jit(solution)/shard_map/while/body/eval_jaxpr/ppermute | solution.py:15
  36.5 4.8 %collective-permute-done = bf16[128,512]{1,0:T(8,128)(2,1)S(1)} collective-permute-done((bf16[128,512]{1,0:T(8,128)(2,1)S(1)}, bf16[128,512]{1,0:T(8,128)(2,1)S(1)}, u32[]{:S(2)}, u32[]{:S(2)}) %collective-permute-start) | collective-permute-done | bytes 131104 | tf_op jit(solution)/shard_map/while/body/eval_jaxpr/ppermute | solution.py:15
  41.2 0.3 fusion.72
  41.6 6.3 %fusion.73 = f32[8,128,128]{1,2,0:T(8,128)S(1)} fusion(bf16[2048,8,128]{0,2,1:T(8,128)(2,1)} %bitcast.117, f32[8]{0:T(128)S(1)} %bitcast.125, bf16[16,8,8,128]{3,2,1,0:T(8,128)(2,1)S(1)} %fusion.72, bf16[2048,1024]{1,0:T(8,128)(2,1)} %get-tuple-element.126), kind=kOutput, calls=%fused_computation.8.clone.1 | convolution fusion | flops 1088421888 | bytes 9175072 | tf_op jit(solution)/shard_map/while/body/eval_jaxpr/phj,jhd->phd/dot_general | solution.py:40
  47.9 3.8 %collective-permute-done.1 = f32[128,1024]{0,1:T(8,128)S(1)} collective-permute-done((f32[128,1024]{0,1:T(8,128)}, f32[128,1024]{0,1:T(8,128)S(1)}, u32[]{:S(2)}, u32[]{:S(2)}) %collective-permute-start.1) | collective-permute-done | bytes 524320 | tf_op jit(solution)/shard_map/while/body/eval_jaxpr/ppermute | solution.py:15
  51.6 0.9 bitcast_add_fusion.2
  52.5 0.0 collective-permute-start
  52.5 1.3 collective-permute-start.1
  53.8 6.9 %collective-permute-done = bf16[128,512]{1,0:T(8,128)(2,1)S(1)} collective-permute-done((bf16[128,512]{1,0:T(8,128)(2,1)S(1)}, bf16[128,512]{1,0:T(8,128)(2,1)S(1)}, u32[]{:S(2)}, u32[]{:S(2)}) %collective-permute-start) | collective-permute-done | bytes 131104 | tf_op jit(solution)/shard_map/while/body/eval_jaxpr/ppermute | solution.py:15
  60.7 0.3 fusion.72
  61.1 6.3 %fusion.73 = f32[8,128,128]{1,2,0:T(8,128)S(1)} fusion(bf16[2048,8,128]{0,2,1:T(8,128)(2,1)} %bitcast.117, f32[8]{0:T(128)S(1)} %bitcast.125, bf16[16,8,8,128]{3,2,1,0:T(8,128)(2,1)S(1)} %fusion.72, bf16[2048,1024]{1,0:T(8,128)(2,1)} %get-tuple-element.126), kind=kOutput, calls=%fused_computation.8.clone.1 | convolution fusion | flops 1088421888 | bytes 9175072 | tf_op jit(solution)/shard_map/while/body/eval_jaxpr/phj,jhd->phd/dot_general | solution.py:40
  67.4 2.9 %collective-permute-done.1 = f32[128,1024]{0,1:T(8,128)S(1)} collective-permute-done((f32[128,1024]{0,1:T(8,128)}, f32[128,1024]{0,1:T(8,128)S(1)}, u32[]{:S(2)}, u32[]{:S(2)}) %collective-permute-start.1) | collective-permute-done | bytes 524320 | tf_op jit(solution)/shard_map/while/body/eval_jaxpr/ppermute | solution.py:15
  70.2 0.9 bitcast_add_fusion.2
  71.1 0.0 collective-permute-start
  71.1 0.0 collective-permute-start.1
  71.1 8.2 %collective-permute-done = bf16[128,512]{1,0:T(8,128)(2,1)S(1)} collective-permute-done((bf16[128,512]{1,0:T(8,128)(2,1)S(1)}, bf16[128,512]{1,0:T(8,128)(2,1)S(1)}, u32[]{:S(2)}, u32[]{:S(2)}) %collective-permute-start) | collective-permute-done | bytes 131104 | tf_op jit(solution)/shard_map/while/body/eval_jaxpr/ppermute | solution.py:15
  79.3 0.3 fusion.72
  79.7 6.3 %fusion.73 = f32[8,128,128]{1,2,0:T(8,128)S(1)} fusion(bf16[2048,8,128]{0,2,1:T(8,128)(2,1)} %bitcast.117, f32[8]{0:T(128)S(1)} %bitcast.125, bf16[16,8,8,128]{3,2,1,0:T(8,128)(2,1)S(1)} %fusion.72, bf16[2048,1024]{1,0:T(8,128)(2,1)} %get-tuple-element.126), kind=kOutput, calls=%fused_computation.8.clone.1 | convolution fusion | flops 1088421888 | bytes 9175072 | tf_op jit(solution)/shard_map/while/body/eval_jaxpr/phj,jhd->phd/dot_general | solution.py:40
  86.0 2.0 %collective-permute-done.1 = f32[128,1024]{0,1:T(8,128)S(1)} collective-permute-done((f32[128,1024]{0,1:T(8,128)}, f32[128,1024]{0,1:T(8,128)S(1)}, u32[]{:S(2)}, u32[]{:S(2)}) %collective-permute-start.1) | collective-permute-done | bytes 524320 | tf_op jit(solution)/shard_map/while/body/eval_jaxpr/ppermute | solution.py:15
  87.9 0.9 bitcast_add_fusion.2
  88.8 0.0 copy-start.6
  88.8 0.0 copy-start.5
  88.8 2.2 %fusion.36 = f32[128,512]{1,0:T(8,128)S(1)} fusion(f32[128,1024]{0,1:T(8,128)} %get-tuple-element.39, bf16[1024,512]{1,0:T(8,128)(2,1)} %param.22), kind=kOutput, calls=%fused_computation.49 | convolution fusion | flops 805306368 | bytes 1835008 | tf_op jit(solution)/shard_map/dot_general | solution.py:86
  91.0 9.5 %all_to_all.10 = f32[4,32,512]{2,1,0:T(8,128)S(1)} all-to-all(f32[4,32,512]{2,1,0:T(8,128)S(1)} %bitcast.119), channel_id=1, replica_groups=mesh['groups'=2,'obs'=4,'hid'=2,'rep'=2] {'obs'}, dimensions={0} | all-to-all | bytes 524288 | tf_op jit(solution)/shard_map/all_to_all | solution.py:90
  100.5 3.4 %all-to-all-start = ((f32[4,32,512]{2,1,0:T(8,128)}), f32[4,32,512]{2,1,0:T(8,128)S(1)}, u32[]{:S(2)}, u32[]{:S(2)}) async-start(f32[4,32,512]{2,1,0:T(8,128)} %bitcast.120), calls=%async_computation | async-start | bytes 524288 | tf_op jit(solution)/shard_map/all_to_all | solution.py:69
  103.9 0.0 all-reduce.2.cloned.1.call-start
  103.9 1.2 fusion.37
  105.2 5.4 %all-to-all-done = f32[4,32,512]{2,1,0:T(8,128)S(1)} async-done(((f32[4,32,512]{2,1,0:T(8,128)}), f32[4,32,512]{2,1,0:T(8,128)S(1)}, u32[]{:S(2)}, u32[]{:S(2)}) %all-to-all-start) | async-done | bytes 262176 | tf_op jit(solution)/shard_map/all_to_all | solution.py:69
  110.6 0.0 copy-done.6
  110.6 1.7 %fusion.23 = f32[128,512]{1,0:T(8,128)S(1)} fusion(f32[128,512]{1,0:T(8,128)S(1)} %bitcast.121, s32[]{:T(128)S(6)} %select_n.2, bf16[1024,512]{1,0:T(8,128)(2,1)S(1)} %copy-done.6, bf16[512,1024]{1,0:T(8,128)(2,1)} %param.23, f32[1024]{0:T(1024)S(1)} %bitcast.123, f32[128,512]{1,0:T(8,128)S(1)} %bitcast.118), kind=kOutput, calls=%fused_computation.30 | convolution fusion | flops 134676480 | bytes 2429952 | tf_op jit(solution)/shard_map/dot_general | solution.py:100
  112.4 0.0 copy-start.3
  112.4 0.7 copy-done.3
  113.1 0.0 all-reduce.2.cloned.1.call-update
  113.2 31.3 %all-reduce.2.cloned.1.call-done = f32[4,32,512]{2,1,0:T(8,128)} async-done(((f32[4,32,512]{2,1,0:T(8,128)}), f32[4,32,512]{2,1,0:T(8,128)}) %all-reduce.2.cloned.1.call-update) | async-done | bytes 262160 | tf_op jit(solution)/shard_map/psum | solution.py:107
  144.5 0.0 copy-done.5
  144.5 1.7 %multiply_add_fusion = f32[4,32,512]{2,1,0:T(8,128)} fusion(f32[4,32,512]{2,1,0:T(8,128)S(1)} %copy-done.5, f32[4,32,512]{2,1,0:T(8,128)S(1)} %all-to-all-done, f32[4,32,512]{2,1,0:T(8,128)} %all-reduce.2.cloned.1.call-done, f32[]{:T(128)S(6)} %sqrt.3, f32[]{:T(128)} %bitcast.6), kind=kLoop, calls=%fused_computation.34 | loop fusion | flops 262144 | bytes 1048584 | tf_op jit(solution)/shard_map/add | solution.py:108
  146.2 1.7 %copy.57 = f32[4,32,512]{2,1,0:T(8,128)} copy(f32[4,32,512]{2,1,0:T(8,128)} %all-reduce.2.cloned.1.call-done) | data formatting | bytes 524288
  (10 shorter events, 0.2 us)
Async XLA Ops:
  7.2 1.2 copy-start
  8.4 4.4 %copy-start.4 = (bf16[256,1024]{1,0:T(8,128)(2,1)S(1)}, bf16[256,1024]{1,0:T(8,128)(2,1)}, u32[]{:S(2)}) copy-start(bf16[256,1024]{1,0:T(8,128)(2,1)} %param.19) | copy-start | bytes 1572868
  12.8 3.3 %copy-start.2 = (f32[1,128,512]{2,1,0:T(8,128)S(1)}, f32[1,128,512]{2,1,0:T(8,128)}, u32[]{:S(2)}) copy-start(f32[1,128,512]{2,1,0:T(8,128)} %param.14) | copy-start | bytes 786436
  16.1 6.5 %copy-start.7 = (bf16[256,8]{0,1:T(8,128)(2,1)S(1)}, bf16[256,8]{0,1:T(8,128)(2,1)}, u32[]{:S(2)}) copy-start(bf16[256,8]{0,1:T(8,128)(2,1)} %param.21) | copy-start | bytes 12292
  16.1 6.6 %copy-start.1 = (bf16[512,1024]{1,0:T(8,128)(2,1)S(1)}, bf16[512,1024]{1,0:T(8,128)(2,1)}, u32[]{:S(2)}) copy-start(bf16[512,1024]{1,0:T(8,128)(2,1)} %param.18) | copy-start | bytes 3145732
  31.9 9.4 %collective-permute-start = (bf16[128,512]{1,0:T(8,128)(2,1)S(1)}, bf16[128,512]{1,0:T(8,128)(2,1)S(1)}, u32[]{:S(2)}, u32[]{:S(2)}) collective-permute-start(bf16[128,512]{1,0:T(8,128)(2,1)S(1)} %get-tuple-element.115), channel_id=1, source_target_pairs={{0,4},{4,8},{8,12},{12,0},{1,5},{5,9},{9,13},{13,1},{2,6},{6,10},{... | collective-permute-start | bytes 393224 | tf_op jit(solution)/shard_map/while/body/eval_jaxpr/ppermute | solution.py:15
  34.9 16.7 %collective-permute-start.1 = (f32[128,1024]{0,1:T(8,128)}, f32[128,1024]{0,1:T(8,128)S(1)}, u32[]{:S(2)}, u32[]{:S(2)}) collective-permute-start(f32[128,1024]{0,1:T(8,128)} %get-tuple-element.116), channel_id=1, source_target_pairs={{0,4},{4,8},{8,12},{12,0},{1,5},{5,9},{9,13},{13,1},{2,6},{6,10},{... | collective-permute-start | bytes 1572872 | tf_op jit(solution)/shard_map/while/body/eval_jaxpr/ppermute | solution.py:15
  52.5 8.2 %collective-permute-start = (bf16[128,512]{1,0:T(8,128)(2,1)S(1)}, bf16[128,512]{1,0:T(8,128)(2,1)S(1)}, u32[]{:S(2)}, u32[]{:S(2)}) collective-permute-start(bf16[128,512]{1,0:T(8,128)(2,1)S(1)} %get-tuple-element.115), channel_id=1, source_target_pairs={{0,4},{4,8},{8,12},{12,0},{1,5},{5,9},{9,13},{13,1},{2,6},{6,10},{... | collective-permute-start | bytes 393224 | tf_op jit(solution)/shard_map/while/body/eval_jaxpr/ppermute | solution.py:15
  52.5 17.7 %collective-permute-start.1 = (f32[128,1024]{0,1:T(8,128)}, f32[128,1024]{0,1:T(8,128)S(1)}, u32[]{:S(2)}, u32[]{:S(2)}) collective-permute-start(f32[128,1024]{0,1:T(8,128)} %get-tuple-element.116), channel_id=1, source_target_pairs={{0,4},{4,8},{8,12},{12,0},{1,5},{5,9},{9,13},{13,1},{2,6},{6,10},{... | collective-permute-start | bytes 1572872 | tf_op jit(solution)/shard_map/while/body/eval_jaxpr/ppermute | solution.py:15
  71.1 8.2 %collective-permute-start = (bf16[128,512]{1,0:T(8,128)(2,1)S(1)}, bf16[128,512]{1,0:T(8,128)(2,1)S(1)}, u32[]{:S(2)}, u32[]{:S(2)}) collective-permute-start(bf16[128,512]{1,0:T(8,128)(2,1)S(1)} %get-tuple-element.115), channel_id=1, source_target_pairs={{0,4},{4,8},{8,12},{12,0},{1,5},{5,9},{9,13},{13,1},{2,6},{6,10},{... | collective-permute-start | bytes 393224 | tf_op jit(solution)/shard_map/while/body/eval_jaxpr/ppermute | solution.py:15
  71.1 16.8 %collective-permute-start.1 = (f32[128,1024]{0,1:T(8,128)}, f32[128,1024]{0,1:T(8,128)S(1)}, u32[]{:S(2)}, u32[]{:S(2)}) collective-permute-start(f32[128,1024]{0,1:T(8,128)} %get-tuple-element.116), channel_id=1, source_target_pairs={{0,4},{4,8},{8,12},{12,0},{1,5},{5,9},{9,13},{13,1},{2,6},{6,10},{... | collective-permute-start | bytes 1572872 | tf_op jit(solution)/shard_map/while/body/eval_jaxpr/ppermute | solution.py:15
  88.8 21.9 %copy-start.6 = (bf16[1024,512]{1,0:T(8,128)(2,1)S(1)}, bf16[1024,512]{1,0:T(8,128)(2,1)}, u32[]{:S(2)}) copy-start(bf16[1024,512]{1,0:T(8,128)(2,1)} %param.25) | copy-start | bytes 3145732
  88.8 55.7 %copy-start.5 = (f32[4,32,512]{2,1,0:T(8,128)S(1)}, f32[4,32,512]{2,1,0:T(8,128)}, u32[]{:S(2)}) copy-start(f32[4,32,512]{2,1,0:T(8,128)} %param.17) | copy-start | bytes 786436
  100.5 10.2 %all-to-all-start = ((f32[4,32,512]{2,1,0:T(8,128)}), f32[4,32,512]{2,1,0:T(8,128)S(1)}, u32[]{:S(2)}, u32[]{:S(2)}) async-start(f32[4,32,512]{2,1,0:T(8,128)} %bitcast.120), calls=%async_computation | async-start | bytes 524288 | tf_op jit(solution)/shard_map/all_to_all | solution.py:69
  103.9 40.6 %all-reduce.2.cloned.1.call-start = ((), (), s32[]{:S(2)}) async-start(), calls=%async_computation.2 | async-start | bytes 524288 | tf_op jit(solution)/shard_map/psum | solution.py:107
  112.4 0.7 copy-start.3
Sparse Core Ops, SparseCore 0:
  113.2 31.2 all-reduce.1
where the time goes:
time: 155 us
  waiting for transfers between devices  65.3 us (42%)
  matrix products  41.7 us (27%)
  between operations  15.1 us (10%)
  blocking collectives  9.51 us (6%)
  starting transfers between devices  9.34 us (6%)
  local copies, waits for them, and re-layouts  9.31 us (6%)
  other arithmetic  4.42 us (3%)
    psum x1, waiting for transfers between devices, on_device(): lax.psum(scores_flat, ('hid', 'rep')).reshape(obs_count, stripe, width)  31.3 us
    ppermute x6, waiting for transfers between devices, passed_along(): lax.ppermute(shard, axis, [(i, (i + by) % size) for i in range(size)])  28.5 us
    dot_general x4, matrix products, pair_pool(): jnp.einsum('phj,jhd->phd', weights, value_heads, preferred_element_type=j...  27.6 us
    all_to_all x1, blocking collectives, on_device(): lax.all_to_all(pieces, 'obs', split_axis=0, concat_axis=0, tiled=True)  9.51 us
    while x1, local copies, waits for them, and re-layouts, on_device(): cycle_state = lax.fori_loop(0, obs_count - 1, turn, (moving, pool(moving)))  6.51 us
    ppermute x6, starting transfers between devices, passed_along(): lax.ppermute(shard, axis, [(i, (i + by) % size) for i in range(size)])  5.89 us
    all_to_all x1, waiting for transfers between devices, on_device(): lax.all_to_all(owned, 'obs', split_axis=0, concat_axis=0, tiled=True)  5.4 us
    dot_general x1, matrix products, on_device(): jnp.dot(obs_embed, w_value, preferred_element_type=jnp.float32)  4.35 us
  transfers between devices with their start and end apart: 8, of which 8 were waited for; matrix products, arithmetic and copies ran while one was open for 14% of the time, Pallas kernels for 0%

commit v1 on v0

--- a/solution.py
+++ b/solution.py
@@ -104,7 +104,7 @@
     scores_flat = lax.dynamic_update_slice_in_dim(
         scores_flat, current - (total_count - 1) * prior_part, start, 0
     )
-    score_total = lax.psum(scores_flat, ("hid", "rep")).reshape(obs_count, stripe, width)
+    score_total = lax.psum(lax.psum(scores_flat, "rep"), "hid").reshape(obs_count, stripe, width)
     updated = theta_owner + delta * score_total + jnp.sqrt(delta) * noise
     return (updated, score_total)
 

time: 155 us -> 168 us (1.084)
  waiting for transfers between devices: 65.3 us -> 78.3 us
    psum x1 -> x2, waiting for transfers between devices: 31.3 us -> 44.3 us  [the longest x1 26.6 us: on_device(): lax.psum(lax.psum(scores_flat, 'rep'), 'hid')]
  transfers between devices with their start and end apart: 8 -> 9, of which waited for: 8 -> 9; matrix products, arithmetic and copies ran while one was open for 14% -> 13% of each run, Pallas kernels for 0% -> 0%
where the time goes in v1:
time: 168 us
  waiting for transfers between devices  78.3 us (47%)
  matrix products  41.7 us (25%)
  between operations  15.1 us (9%)
  blocking collectives  9.51 us (6%)
  starting transfers between devices  9.39 us (6%)
  local copies, waits for them, and re-layouts  9.31 us (6%)
  other arithmetic  4.42 us (3%)
    ppermute x6, waiting for transfers between devices, passed_along(): lax.ppermute(shard, axis, [(i, (i + by) % size) for i in range(size)])  28.5 us
    dot_general x4, matrix products, pair_pool(): jnp.einsum('phj,jhd->phd', weights, value_heads, preferred_element_type=j...  27.6 us
    psum x1, waiting for transfers between devices, on_device(): lax.psum(lax.psum(scores_flat, 'rep'), 'hid')  26.6 us
    psum x1, waiting for transfers between devices, on_device(): lax.psum(scores_flat, 'rep')  17.7 us
    all_to_all x1, blocking collectives, on_device(): lax.all_to_all(pieces, 'obs', split_axis=0, concat_axis=0, tiled=True)  9.51 us
    while x1, local copies, waits for them, and re-layouts, on_device(): cycle_state = lax.fori_loop(0, obs_count - 1, turn, (moving, pool(moving)))  6.51 us
    ppermute x6, starting transfers between devices, passed_along(): lax.ppermute(shard, axis, [(i, (i + by) % size) for i in range(size)])  5.89 us
    all_to_all x1, waiting for transfers between devices, on_device(): lax.all_to_all(owned, 'obs', split_axis=0, concat_axis=0, tiled=True)  5.4 us
  transfers between devices with their start and end apart: 9, of which 9 were waited for; matrix products, arithmetic and copies ran while one was open for 13% of the time, Pallas kernels for 0%

profile of v1, /device:TPU:0, one launch (start us, length us, event | category | flops | bytes accessed | tf_op | source)
XLA Modules:
  0.0 167.8 jit_solution(16154696894718025608)
XLA Ops:
  7.2 0.0 copy-start
  8.1 0.3 copy-done
  8.4 0.0 copy-start.4
  8.4 4.3 %convolution_convert_fusion.2 = bf16[2048,1024]{0,1:T(8,128)(2,1)} fusion(bf16[2048,256]{1,0:T(8,128)(2,1)S(1)} %copy-done, bf16[256,1024]{1,0:T(8,128)(2,1)} %param.20), kind=kOutput, calls=%fused_computation.23 | convolution fusion | flops 1075838976 | bytes 5767168 | tf_op jit(solution)/shard_map/dot_general | solution.py:63
  12.8 0.0 copy-done.4
  12.8 0.0 copy-start.2
  12.8 3.3 %convolution_convert_fusion.1 = bf16[2048,1024]{0,1:T(8,128)(2,1)} fusion(bf16[2048,256]{1,0:T(8,128)(2,1)S(1)} %copy-done, bf16[256,1024]{1,0:T(8,128)(2,1)S(1)} %copy-done.4), kind=kOutput, calls=%fused_computation.22 | convolution fusion | flops 1075838976 | bytes 5767168 | tf_op jit(solution)/shard_map/dot_general | solution.py:62
  16.0 0.0 copy-done.2
  16.1 0.0 copy-start.7
  16.1 0.0 copy-start.1
  16.1 6.5 %copy.19 = bf16[2048,1024]{1,0:T(8,128)(2,1)} copy(bf16[2048,1024]{0,1:T(8,128)(2,1)} %convolution_convert_fusion.1) | data formatting | bytes 8388608 | tf_op jit(solution)/shard_map/while | solution.py:83
  22.6 0.0 copy-done.7
  22.6 0.1 fusion.35
  22.7 0.0 copy-done.1
  22.7 0.3 fusion.21
  23.0 8.8 %fusion.20 = f32[8,128,128]{2,1,0:T(8,128)} fusion(bf16[2048,8,128]{0,2,1:T(8,128)(2,1)} %bitcast.116, bf16[2048,8,128]{0,2,1:T(8,128)(2,1)} %bitcast.115, f32[8]{0:T(128)S(1)} %bitcast.124, bf16[16,8,8,128]{3,2,1,0:T(8,128)(2,1)S(1)} %fusion.21), kind=kOutput, calls=%fused_computation.24 | convolution fusion | flops 1088421888 | bytes 9175072 | tf_op jit(solution)/shard_map/phj,jhd->phd/dot_general | solution.py:40
  31.9 56.9 %while.12 = (s32[]{:T(128)}, bf16[128,512]{1,0:T(8,128)(2,1)S(1)}, f32[128,1024]{0,1:T(8,128)}, bf16[512,1024]{1,0:T(8,128)(2,1)S(1)}, bf16[2048,1024]{1,0:T(8,1...) while((s32[]{:T(128)}, bf16[128,512]{1,0:T(8,128)(2,1)S(1)}, ...), condition=%wide.region_1.2_spmd, body=%wide.region_0.1_spmd.sunk | while | flops 1222901760 | bytes 15073477 | solution.py:83
  31.9 3.0 %collective-permute-start = (bf16[128,512]{1,0:T(8,128)(2,1)S(1)}, bf16[128,512]{1,0:T(8,128)(2,1)S(1)}, u32[]{:S(2)}, u32[]{:S(2)}) collective-permute-start(bf16[128,512]{1,0:T(8,128)(2,1)S(1)} %get-tuple-element.115), channel_id=1, source_target_pairs={{0,4},{4,8},{8,12},{12,0},{1,5},{5,9},{9,13},{13,1},{2,6},{6,10},{... | collective-permute-start | bytes 393224 | tf_op jit(solution)/shard_map/while/body/eval_jaxpr/ppermute | solution.py:15
  34.9 1.6 collective-permute-start.1
  36.5 4.8 %collective-permute-done = bf16[128,512]{1,0:T(8,128)(2,1)S(1)} collective-permute-done((bf16[128,512]{1,0:T(8,128)(2,1)S(1)}, bf16[128,512]{1,0:T(8,128)(2,1)S(1)}, u32[]{:S(2)}, u32[]{:S(2)}) %collective-permute-start) | collective-permute-done | bytes 131104 | tf_op jit(solution)/shard_map/while/body/eval_jaxpr/ppermute | solution.py:15
  41.2 0.3 fusion.72
  41.6 6.3 %fusion.73 = f32[8,128,128]{1,2,0:T(8,128)S(1)} fusion(bf16[2048,8,128]{0,2,1:T(8,128)(2,1)} %bitcast.117, f32[8]{0:T(128)S(1)} %bitcast.125, bf16[16,8,8,128]{3,2,1,0:T(8,128)(2,1)S(1)} %fusion.72, bf16[2048,1024]{1,0:T(8,128)(2,1)} %get-tuple-element.126), kind=kOutput, calls=%fused_computation.8.clone.1 | convolution fusion | flops 1088421888 | bytes 9175072 | tf_op jit(solution)/shard_map/while/body/eval_jaxpr/phj,jhd->phd/dot_general | solution.py:40
  47.9 3.8 %collective-permute-done.1 = f32[128,1024]{0,1:T(8,128)S(1)} collective-permute-done((f32[128,1024]{0,1:T(8,128)}, f32[128,1024]{0,1:T(8,128)S(1)}, u32[]{:S(2)}, u32[]{:S(2)}) %collective-permute-start.1) | collective-permute-done | bytes 524320 | tf_op jit(solution)/shard_map/while/body/eval_jaxpr/ppermute | solution.py:15
  51.6 0.9 bitcast_add_fusion.2
  52.5 0.0 collective-permute-start
  52.5 1.3 collective-permute-start.1
  53.8 6.9 %collective-permute-done = bf16[128,512]{1,0:T(8,128)(2,1)S(1)} collective-permute-done((bf16[128,512]{1,0:T(8,128)(2,1)S(1)}, bf16[128,512]{1,0:T(8,128)(2,1)S(1)}, u32[]{:S(2)}, u32[]{:S(2)}) %collective-permute-start) | collective-permute-done | bytes 131104 | tf_op jit(solution)/shard_map/while/body/eval_jaxpr/ppermute | solution.py:15
  60.7 0.3 fusion.72
  61.1 6.3 %fusion.73 = f32[8,128,128]{1,2,0:T(8,128)S(1)} fusion(bf16[2048,8,128]{0,2,1:T(8,128)(2,1)} %bitcast.117, f32[8]{0:T(128)S(1)} %bitcast.125, bf16[16,8,8,128]{3,2,1,0:T(8,128)(2,1)S(1)} %fusion.72, bf16[2048,1024]{1,0:T(8,128)(2,1)} %get-tuple-element.126), kind=kOutput, calls=%fused_computation.8.clone.1 | convolution fusion | flops 1088421888 | bytes 9175072 | tf_op jit(solution)/shard_map/while/body/eval_jaxpr/phj,jhd->phd/dot_general | solution.py:40
  67.4 2.9 %collective-permute-done.1 = f32[128,1024]{0,1:T(8,128)S(1)} collective-permute-done((f32[128,1024]{0,1:T(8,128)}, f32[128,1024]{0,1:T(8,128)S(1)}, u32[]{:S(2)}, u32[]{:S(2)}) %collective-permute-start.1) | collective-permute-done | bytes 524320 | tf_op jit(solution)/shard_map/while/body/eval_jaxpr/ppermute | solution.py:15
  70.2 0.9 bitcast_add_fusion.2
  71.1 0.0 collective-permute-start
  71.1 0.0 collective-permute-start.1
  71.1 8.2 %collective-permute-done = bf16[128,512]{1,0:T(8,128)(2,1)S(1)} collective-permute-done((bf16[128,512]{1,0:T(8,128)(2,1)S(1)}, bf16[128,512]{1,0:T(8,128)(2,1)S(1)}, u32[]{:S(2)}, u32[]{:S(2)}) %collective-permute-start) | collective-permute-done | bytes 131104 | tf_op jit(solution)/shard_map/while/body/eval_jaxpr/ppermute | solution.py:15
  79.3 0.3 fusion.72
  79.7 6.3 %fusion.73 = f32[8,128,128]{1,2,0:T(8,128)S(1)} fusion(bf16[2048,8,128]{0,2,1:T(8,128)(2,1)} %bitcast.117, f32[8]{0:T(128)S(1)} %bitcast.125, bf16[16,8,8,128]{3,2,1,0:T(8,128)(2,1)S(1)} %fusion.72, bf16[2048,1024]{1,0:T(8,128)(2,1)} %get-tuple-element.126), kind=kOutput, calls=%fused_computation.8.clone.1 | convolution fusion | flops 1088421888 | bytes 9175072 | tf_op jit(solution)/shard_map/while/body/eval_jaxpr/phj,jhd->phd/dot_general | solution.py:40
  86.0 2.0 %collective-permute-done.1 = f32[128,1024]{0,1:T(8,128)S(1)} collective-permute-done((f32[128,1024]{0,1:T(8,128)}, f32[128,1024]{0,1:T(8,128)S(1)}, u32[]{:S(2)}, u32[]{:S(2)}) %collective-permute-start.1) | collective-permute-done | bytes 524320 | tf_op jit(solution)/shard_map/while/body/eval_jaxpr/ppermute | solution.py:15
  87.9 0.9 bitcast_add_fusion.2
  88.8 0.0 copy-start.6
  88.8 0.0 copy-start.5
  88.8 2.2 %fusion.36 = f32[128,512]{1,0:T(8,128)S(1)} fusion(f32[128,1024]{0,1:T(8,128)} %get-tuple-element.39, bf16[1024,512]{1,0:T(8,128)(2,1)} %param.22), kind=kOutput, calls=%fused_computation.49 | convolution fusion | flops 805306368 | bytes 1835008 | tf_op jit(solution)/shard_map/dot_general | solution.py:86
  91.0 9.5 %all_to_all.10 = f32[4,32,512]{2,1,0:T(8,128)S(1)} all-to-all(f32[4,32,512]{2,1,0:T(8,128)S(1)} %bitcast.119), channel_id=1, replica_groups=mesh['groups'=2,'obs'=4,'hid'=2,'rep'=2] {'obs'}, dimensions={0} | all-to-all | bytes 524288 | tf_op jit(solution)/shard_map/all_to_all | solution.py:90
  100.5 3.4 %all-to-all-start = ((f32[4,32,512]{2,1,0:T(8,128)}), f32[4,32,512]{2,1,0:T(8,128)S(1)}, u32[]{:S(2)}, u32[]{:S(2)}) async-start(f32[4,32,512]{2,1,0:T(8,128)} %bitcast.120), calls=%async_computation | async-start | bytes 524288 | tf_op jit(solution)/shard_map/all_to_all | solution.py:69
  103.9 0.0 all-reduce.3.cloned.1.call-start
  103.9 1.2 fusion.37
  105.2 5.4 %all-to-all-done = f32[4,32,512]{2,1,0:T(8,128)S(1)} async-done(((f32[4,32,512]{2,1,0:T(8,128)}), f32[4,32,512]{2,1,0:T(8,128)S(1)}, u32[]{:S(2)}, u32[]{:S(2)}) %all-to-all-start) | async-done | bytes 262176 | tf_op jit(solution)/shard_map/all_to_all | solution.py:69
  110.6 0.0 copy-done.6
  110.6 1.7 %fusion.23 = f32[128,512]{1,0:T(8,128)S(1)} fusion(f32[128,512]{1,0:T(8,128)S(1)} %bitcast.121, s32[]{:T(128)S(6)} %select_n.2, bf16[1024,512]{1,0:T(8,128)(2,1)S(1)} %copy-done.6, bf16[512,1024]{1,0:T(8,128)(2,1)} %param.23, f32[1024]{0:T(1024)S(1)} %bitcast.123, f32[128,512]{1,0:T(8,128)S(1)} %bitcast.118), kind=kOutput, calls=%fused_computation.30 | convolution fusion | flops 134676480 | bytes 2429952 | tf_op jit(solution)/shard_map/dot_general | solution.py:100
  112.4 0.0 copy-start.3
  112.4 0.7 copy-done.3
  113.1 0.0 all-reduce.3.cloned.1.call-update
  113.1 0.0 all-reduce.5.cloned.1.call-start
  113.1 17.7 %all-reduce.3.cloned.1.call-done = f32[128,512]{1,0:T(8,128)} async-done(((f32[128,512]{1,0:T(8,128)}), f32[128,512]{1,0:T(8,128)}) %all-reduce.3.cloned.1.call-update) | async-done | bytes 262160 | tf_op jit(solution)/shard_map/psum | solution.py:107
  130.8 0.0 all-reduce.5.cloned.1.call-update
  130.9 26.6 %all-reduce.5.cloned.1.call-done = f32[4,32,512]{2,1,0:T(8,128)} async-done(((f32[4,32,512]{2,1,0:T(8,128)}), f32[4,32,512]{2,1,0:T(8,128)}) %all-reduce.5.cloned.1.call-update) | async-done | bytes 262160 | tf_op jit(solution)/shard_map/psum | solution.py:107
  157.6 0.0 copy-done.5
  157.6 1.7 %multiply_add_fusion = f32[4,32,512]{2,1,0:T(8,128)} fusion(f32[4,32,512]{2,1,0:T(8,128)S(1)} %copy-done.5, f32[4,32,512]{2,1,0:T(8,128)S(1)} %all-to-all-done, f32[4,32,512]{2,1,0:T(8,128)} %all-reduce.5.cloned.1.call-done, f32[]{:T(128)S(6)} %sqrt.3, f32[]{:T(128)} %bitcast.6), kind=kLoop, calls=%fused_computation.34 | loop fusion | flops 262144 | bytes 1048584 | tf_op jit(solution)/shard_map/add | solution.py:108
  159.3 1.7 copy.58
  (10 shorter events, 0.2 us)
Async XLA Ops:
  7.2 1.2 copy-start
  8.4 4.4 %copy-start.4 = (bf16[256,1024]{1,0:T(8,128)(2,1)S(1)}, bf16[256,1024]{1,0:T(8,128)(2,1)}, u32[]{:S(2)}) copy-start(bf16[256,1024]{1,0:T(8,128)(2,1)} %param.19) | copy-start | bytes 1572868
  12.8 3.3 %copy-start.2 = (f32[1,128,512]{2,1,0:T(8,128)S(1)}, f32[1,128,512]{2,1,0:T(8,128)}, u32[]{:S(2)}) copy-start(f32[1,128,512]{2,1,0:T(8,128)} %param.14) | copy-start | bytes 786436
  16.1 6.5 %copy-start.7 = (bf16[256,8]{0,1:T(8,128)(2,1)S(1)}, bf16[256,8]{0,1:T(8,128)(2,1)}, u32[]{:S(2)}) copy-start(bf16[256,8]{0,1:T(8,128)(2,1)} %param.21) | copy-start | bytes 12292
  16.1 6.6 %copy-start.1 = (bf16[512,1024]{1,0:T(8,128)(2,1)S(1)}, bf16[512,1024]{1,0:T(8,128)(2,1)}, u32[]{:S(2)}) copy-start(bf16[512,1024]{1,0:T(8,128)(2,1)} %param.18) | copy-start | bytes 3145732
  31.9 9.4 %collective-permute-start = (bf16[128,512]{1,0:T(8,128)(2,1)S(1)}, bf16[128,512]{1,0:T(8,128)(2,1)S(1)}, u32[]{:S(2)}, u32[]{:S(2)}) collective-permute-start(bf16[128,512]{1,0:T(8,128)(2,1)S(1)} %get-tuple-element.115), channel_id=1, source_target_pairs={{0,4},{4,8},{8,12},{12,0},{1,5},{5,9},{9,13},{13,1},{2,6},{6,10},{... | collective-permute-start | bytes 393224 | tf_op jit(solution)/shard_map/while/body/eval_jaxpr/ppermute | solution.py:15
  34.9 16.7 %collective-permute-start.1 = (f32[128,1024]{0,1:T(8,128)}, f32[128,1024]{0,1:T(8,128)S(1)}, u32[]{:S(2)}, u32[]{:S(2)}) collective-permute-start(f32[128,1024]{0,1:T(8,128)} %get-tuple-element.116), channel_id=1, source_target_pairs={{0,4},{4,8},{8,12},{12,0},{1,5},{5,9},{9,13},{13,1},{2,6},{6,10},{... | collective-permute-start | bytes 1572872 | tf_op jit(solution)/shard_map/while/body/eval_jaxpr/ppermute | solution.py:15
  52.5 8.2 %collective-permute-start = (bf16[128,512]{1,0:T(8,128)(2,1)S(1)}, bf16[128,512]{1,0:T(8,128)(2,1)S(1)}, u32[]{:S(2)}, u32[]{:S(2)}) collective-permute-start(bf16[128,512]{1,0:T(8,128)(2,1)S(1)} %get-tuple-element.115), channel_id=1, source_target_pairs={{0,4},{4,8},{8,12},{12,0},{1,5},{5,9},{9,13},{13,1},{2,6},{6,10},{... | collective-permute-start | bytes 393224 | tf_op jit(solution)/shard_map/while/body/eval_jaxpr/ppermute | solution.py:15
  52.5 17.7 %collective-permute-start.1 = (f32[128,1024]{0,1:T(8,128)}, f32[128,1024]{0,1:T(8,128)S(1)}, u32[]{:S(2)}, u32[]{:S(2)}) collective-permute-start(f32[128,1024]{0,1:T(8,128)} %get-tuple-element.116), channel_id=1, source_target_pairs={{0,4},{4,8},{8,12},{12,0},{1,5},{5,9},{9,13},{13,1},{2,6},{6,10},{... | collective-permute-start | bytes 1572872 | tf_op jit(solution)/shard_map/while/body/eval_jaxpr/ppermute | solution.py:15
  71.1 8.2 %collective-permute-start = (bf16[128,512]{1,0:T(8,128)(2,1)S(1)}, bf16[128,512]{1,0:T(8,128)(2,1)S(1)}, u32[]{:S(2)}, u32[]{:S(2)}) collective-permute-start(bf16[128,512]{1,0:T(8,128)(2,1)S(1)} %get-tuple-element.115), channel_id=1, source_target_pairs={{0,4},{4,8},{8,12},{12,0},{1,5},{5,9},{9,13},{13,1},{2,6},{6,10},{... | collective-permute-start | bytes 393224 | tf_op jit(solution)/shard_map/while/body/eval_jaxpr/ppermute | solution.py:15
  71.1 16.8 %collective-permute-start.1 = (f32[128,1024]{0,1:T(8,128)}, f32[128,1024]{0,1:T(8,128)S(1)}, u32[]{:S(2)}, u32[]{:S(2)}) collective-permute-start(f32[128,1024]{0,1:T(8,128)} %get-tuple-element.116), channel_id=1, source_target_pairs={{0,4},{4,8},{8,12},{12,0},{1,5},{5,9},{9,13},{13,1},{2,6},{6,10},{... | collective-permute-start | bytes 1572872 | tf_op jit(solution)/shard_map/while/body/eval_jaxpr/ppermute | solution.py:15
  88.8 21.9 %copy-start.6 = (bf16[1024,512]{1,0:T(8,128)(2,1)S(1)}, bf16[1024,512]{1,0:T(8,128)(2,1)}, u32[]{:S(2)}) copy-start(bf16[1024,512]{1,0:T(8,128)(2,1)} %param.25) | copy-start | bytes 3145732
  88.8 68.8 %copy-start.5 = (f32[4,32,512]{2,1,0:T(8,128)S(1)}, f32[4,32,512]{2,1,0:T(8,128)}, u32[]{:S(2)}) copy-start(f32[4,32,512]{2,1,0:T(8,128)} %param.17) | copy-start | bytes 786436
  100.5 10.2 %all-to-all-start = ((f32[4,32,512]{2,1,0:T(8,128)}), f32[4,32,512]{2,1,0:T(8,128)S(1)}, u32[]{:S(2)}, u32[]{:S(2)}) async-start(f32[4,32,512]{2,1,0:T(8,128)} %bitcast.120), calls=%async_computation | async-start | bytes 524288 | tf_op jit(solution)/shard_map/all_to_all | solution.py:69
  103.9 26.9 %all-reduce.3.cloned.1.call-start = ((), (), s32[]{:S(2)}) async-start(), calls=%async_computation.2 | async-start | bytes 524288 | tf_op jit(solution)/shard_map/psum | solution.py:107
  112.4 0.7 copy-start.3
  113.1 44.5 %all-reduce.5.cloned.1.call-start = ((), (), s32[]{:S(2)}) async-start(), calls=%async_computation.3 | async-start | bytes 524288 | tf_op jit(solution)/shard_map/psum | solution.py:107
Sparse Core Ops, SparseCore 0:
  113.2 17.5 all-reduce.2
  133.2 24.3 all-reduce.4
